TPU v7x, 32 devices: a whole 2x2x4 slice. The times are simulated.
32 devices in a mesh: inner: 8 (over y, x, core), outer: 4 (over z).
Axes of the slice: x: 2, y: 2, z: 4, core: 2. Of those that a mesh axis runs over, the one named last changes fastest.
Arguments:
- coupling: float32 [4, 8, 36, 128, 128], P('outer', 'inner'), may hold values from -0.046875 to 0.046875
- log_diag: float32 [4, 8, 1024], P('outer', 'inner'), may hold values from -0.05 to 0.05
- pattern: int32 [8, 8], replicated, may hold values 0 or 1
- boundary: float32 [1024, 256], replicated, may hold values from -6 to 6
Outputs:
- transported: float32 [4, 8, 1024, 256], P('outer', 'inner')
All inputs are finite; a program needn't handle non-finite values.
Results may differ from a plain program's by a relative error of at most 0.0003.
Values sent between devices are 32-bit elements; how exact they have to be, the bound alone decides.
A program may use at most 192 MiB of HBM per device.

v0:
```python
import jax
import jax.numpy as jnp
import numpy as np
from jax import lax
from jax.sharding import PartitionSpec as P

highest = lax.Precision.HIGHEST


def prefix(part, axis, combine, identity):
    place = lax.axis_index(axis)
    gathered = lax.all_gather(part, axis)
    state = jnp.zeros_like(part) + jnp.asarray(identity, part.dtype)

    def one(step, state):
        return combine(state, lax.dynamic_index_in_dim(gathered, step, 0, False))

    return lax.fori_loop(0, place, one, state)


def broadcast(value, axis, source):
    kept = jnp.where(lax.axis_index(axis) == source, value, 0).astype(value.dtype)
    return lax.psum(kept, axis)


def passed_along(value, axis, steps):
    count = lax.axis_size(axis)
    leading, last = (max(0, -steps), min(count, count - steps))
    return lax.ppermute(value, axis, [(source, source + steps) for source in range(leading, last)])


def packed_start(tile_row):
    return tile_row * (tile_row + 1) // 2


def column_start(tile_col, tile_count):
    return sum((tile_count - earlier_col for earlier_col in range(tile_col)))


def tile_layout(tile_count):
    rows_list = []
    cols_list = []
    for tile_row in range(tile_count):
        for tile_col in range(tile_row + 1):
            rows_list.append(tile_row)
            cols_list.append(tile_col)
    return (np.array(rows_list, dtype=np.int32), np.array(cols_list, dtype=np.int32))


def column_order(tile_count):
    order_list = []
    for tile_col in range(tile_count):
        for tile_row in range(tile_col, tile_count):
            order_list.append(packed_start(tile_row) + tile_col)
    return np.array(order_list, dtype=np.int32)


def propagator(coupling, log_diag, pattern, tile_count):
    row_ids, col_ids = tile_layout(tile_count)
    tile_size = coupling.shape[-1]
    on_diagonal = row_ids == col_ids
    chosen = pattern[row_ids, col_ids]
    weight = jnp.where(on_diagonal, 1, chosen).astype(jnp.float32)
    growth = jnp.exp(log_diag).reshape(tile_count, tile_size)[row_ids]
    identity = jnp.eye(tile_size, dtype=jnp.float32)
    diag_part = jnp.where(on_diagonal[:, None, None], identity[None] * growth[:, None, :], 0.0)
    return coupling * weight[:, None, None] + diag_part


def compose(later_map, earlier, tile_count):
    by_column = earlier[column_order(tile_count)]
    outputs = []
    for tile_row in range(tile_count):
        for tile_col in range(tile_row + 1):
            left_tiles = later_map[
                packed_start(tile_row) + tile_col : packed_start(tile_row) + tile_row + 1
            ]
            first = column_start(tile_col, tile_count)
            right_tiles = by_column[first : first + tile_row - tile_col + 1]
            outputs.append(
                jnp.einsum(
                    "kab,kbc->ac",
                    left_tiles,
                    right_tiles,
                    precision=highest,
                    preferred_element_type=jnp.float32,
                )
            )
    return jnp.stack(outputs)


def apply_packed(matrix, columns, tile_count):
    tile_size = matrix.shape[1]
    stacked = columns.reshape(tile_count, tile_size, columns.shape[-1])
    blocks = []
    for tile_row in range(tile_count):
        row_tiles = matrix[packed_start(tile_row) : packed_start(tile_row) + tile_row + 1]
        blocks.append(
            jnp.einsum(
                "kab,kbc->ac",
                row_tiles,
                stacked[: tile_row + 1],
                precision=highest,
                preferred_element_type=jnp.float32,
            )
        )
    return jnp.concatenate(blocks, axis=0)


def shards(coupling, log_diag, pattern, boundary):
    tile_size = coupling.shape[-1]
    tile_count = boundary.shape[0] // tile_size
    built_maps = propagator(coupling[0, 0], log_diag[0, 0], pattern, tile_count)
    prefixes = [built_maps]
    local_total = prefixes[-1]
    identity_packed = propagator(
        jnp.zeros_like(coupling[0, 0]), jnp.zeros_like(log_diag[0, 0]), pattern, tile_count
    )

    def chain_rule(earlier, later_map):
        return compose(later_map, earlier, tile_count)

    before = prefix(local_total, "inner", chain_rule, identity_packed)
    inner_count = lax.axis_size("inner")
    inclusive = [compose(prefix_now, before, tile_count) for prefix_now in prefixes]
    whole_group = broadcast(inclusive[-1], "inner", inner_count - 1)

    def advance(carry_cols):
        return apply_packed(whole_group, carry_cols, tile_count)

    slice_width = boundary.shape[1] // inner_count
    start_col = lax.axis_index("inner") * slice_width
    own_columns = lax.dynamic_slice_in_dim(boundary, start_col, slice_width, 1)
    outer_place = lax.axis_index("outer")

    def carry_step(step_number, carry_cols):
        outgoing = lax.cond(step_number == outer_place, advance, lambda held: held, carry_cols)
        arrived = passed_along(outgoing, "outer", 1)
        return jnp.where(outer_place == step_number + 1, arrived, carry_cols)

    entering = lax.fori_loop(0, lax.axis_size("outer") - 1, carry_step, own_columns)
    column_piece = lax.all_gather(entering, "inner", axis=1, tiled=True)
    return jnp.stack(
        [apply_packed(prefix_map, column_piece, tile_count) for prefix_map in inclusive]
    )[None]


def solution(mesh):
    return jax.shard_map(
        shards,
        mesh=mesh,
        in_specs=(P("outer", "inner", None, None, None), P("outer", "inner", None), P(), P()),
        out_specs=P("outer", "inner", None, None),
        check_vma=False,
    )
```

profile of v0, /device:TPU:30, one launch (start us, length us, event | category | flops | bytes accessed | tf_op | source)
XLA Modules:
  0.0 814.8 jit_solution(5795419623149166369)
XLA Ops:
  11.1 3.5 fusion.124
  16.2 2.8 fusion.125
  19.1 94.2 %all-gather.3.cloned.1.call-done = f32[8,36,128,128]{3,2,1,0:T(8,128)} async-done(((f32[1,36,128,128]{3,2,1,0:T(8,128)}), f32[8,36,128,128]{3,2,1,0:T(8,128)}) %all-gather.3.cloned.1.call-update) | async-done | bytes 18874384 | tf_op jit(solution)/shard_map/all_gather | solution.py:12
  113.3 422.9 %while.28 = (s32[]{:T(128)}, f32[36,128,128]{2,1,0:T(8,128)}, s32[]{:T(128)}, f32[8,36,128,128]{3,2,1,0:T(8,128)}, s32[]{:T(128)}, /*index=5*/s32[36]{0:T(128)S(...) while((s32[]{:T(128)}, f32[36,128,128]{2,1,0:T(8,128)}, ...), condition=%wide.region_1.2_spmd.clone, body=%wide.region_0.1_spmd.sunk.clone.sunk | while | flops 3019899904 | bytes 22812016 | solution.py:18
  113.3 2.4 gather_fusion
  154.2 2.2 fusion.343
  156.4 2.1 fusion.344
  167.8 2.3 fusion.350
  170.1 2.2 fusion.351
  172.3 2.1 fusion.352
  183.8 2.4 gather_fusion
  224.6 2.2 fusion.343
  226.9 2.1 fusion.344
  238.3 2.3 fusion.350
  240.6 2.2 fusion.351
  242.8 2.1 fusion.352
  254.3 2.4 gather_fusion
  295.1 2.2 fusion.343
  297.3 2.1 fusion.344
  308.8 2.3 fusion.350
  311.1 2.2 fusion.351
  313.3 2.1 fusion.352
  324.8 2.4 gather_fusion
  365.6 2.2 fusion.343
  367.8 2.1 fusion.344
  379.3 2.3 fusion.350
  381.6 2.2 fusion.351
  383.8 2.1 fusion.352
  395.3 2.4 gather_fusion
  436.1 2.2 fusion.343
  438.3 2.1 fusion.344
  449.8 2.3 fusion.350
  452.1 2.2 fusion.351
  454.3 2.1 fusion.352
  465.7 2.4 gather_fusion
  506.6 2.2 fusion.343
  508.8 2.1 fusion.344
  520.2 2.3 fusion.350
  522.5 2.2 fusion.351
  536.2 3.9 gather_fusion.3
  569.7 132.4 %all-reduce.2.cloned.1.call-done = f32[36,128,128]{2,1,0:T(8,128)} async-done(((f32[36,128,128]{2,1,0:T(8,128)}), f32[36,128,128]{2,1,0:T(8,128)}) %all-reduce.2.cloned.1.call-update) | async-done | bytes 2359312 | tf_op jit(solution)/shard_map/psum | solution.py:23
  702.1 58.2 %while.27 = (s32[]{:T(128)}, f32[1024,32]{0,1:T(8,128)S(1)}, s32[]{:T(128)}, f32[36,128,128]{2,1,0:T(8,128)}, s32[]{:T(128)}) while((s32[]{:T(128)}, f32[1024,32]{0,1:T(8,128)S(1)}, s32[]{:T(128)}, f32[36,128,128]{2,1,0:T(8,128)}, s32[]{:T(128)}) %tuple.99), condition=%wide.region_6.7_spmd, body=%wide.region_3.6_spmd.sunk | while | flops 226525184 | bytes 27656368 | solution.py:141
  704.1 5.8 collective-permute-done
  711.9 5.8 collective-permute-done
  719.7 40.6 %collective-permute-done = f32[1024,32]{0,1:T(8,128)S(1)} collective-permute-done((f32[1024,32]{0,1:T(8,128)}, f32[1024,32]{0,1:T(8,128)S(1)}, u32[]{:S(2)}, u32[]{:S(2)}) %collective-permute-start) | collective-permute-done | bytes 131104 | tf_op jit(solution)/shard_map/while/body/eval_jaxpr/ppermute | solution.py:29
  761.0 24.1 %all-gather.5.cloned.1.call-done = f32[1024,256]{0,1:T(8,128)} async-done(((f32[1024,32]{0,1:T(8,128)}), f32[1024,256]{0,1:T(8,128)}) %all-gather.5.cloned.1.call-update) | async-done | bytes 1048592 | tf_op jit(solution)/shard_map/all_gather | solution.py:142
  796.7 2.2 fusion.128
  805.8 2.5 fusion.131
  (318 shorter events, 407.5 us)
Async XLA Ops:
  6.5 562.8 %copy-start = (f32[1024,256]{1,0:T(8,128)S(1)}, f32[1024,256]{1,0:T(8,128)}, u32[]{:S(2)}) copy-start(f32[1024,256]{1,0:T(8,128)} %param.31) | copy-start | bytes 3145732
  6.5 106.8 %all-gather.3.cloned.1.call-start = ((), (), s32[]{:S(2)}) async-start(), calls=%async_computation | async-start | bytes 21233664 | tf_op jit(solution)/shard_map/all_gather | solution.py:12
  14.5 0.7 copy-start.19
  14.5 1.7 copy-start.6
  14.6 687.5 %all-reduce.2.cloned.1.call-start = ((), (), s32[]{:S(2)}) async-start(), calls=%async_computation.1 | async-start | bytes 4718592 | tf_op jit(solution)/shard_map/psum | solution.py:23
  16.2 97.1 %copy-start.18 = (s32[36]{0:T(128)S(1)}, s32[36]{0:T(128)}, u32[]{:S(2)}) copy-start(s32[36]{0:T(128)} %constant.100) | copy-start | bytes 436
  536.2 3.9 copy-start.3
  540.1 10.6 %copy-start.4 = (f32[36,128,128]{2,1,0:T(8,128)S(1)}, f32[36,128,128]{2,1,0:T(8,128)}, u32[]{:S(2)}) copy-start(f32[36,128,128]{2,1,0:T(8,128)} %gather_fusion.3) | copy-start | bytes 7077892
  556.0 0.7 copy-start.16
  558.9 0.8 copy-start.14
  562.4 0.8 copy-start.12
  566.9 0.8 copy-start.10
  569.3 215.8 %all-gather.5.cloned.1.call-start = ((), (), s32[]{:S(2)}) async-start(), calls=%async_computation.2 | async-start | bytes 1179648 | tf_op jit(solution)/shard_map/all_gather | solution.py:142
  702.8 7.1 collective-permute-start
  710.6 7.1 collective-permute-start
  718.4 41.9 %collective-permute-start = (f32[1024,32]{0,1:T(8,128)}, f32[1024,32]{0,1:T(8,128)S(1)}, u32[]{:S(2)}, u32[]{:S(2)}) collective-permute-start(f32[1024,32]{0,1:T(8,128)} %get-tuple-element.440), channel_id=1, source_target_pairs={{0,1},{1,2},{2,3},{4,5},{5,6},{6,7},{8,9},{9,10},{10,11},{12,13},{... | collective-permute-start | bytes 393224 | tf_op jit(solution)/shard_map/while/body/eval_jaxpr/ppermute | solution.py:29
  760.3 0.7 copy-start.2
  785.0 3.9 slice-start
  786.9 2.2 slice-start.1
  789.2 1.1 slice-start.2
  790.3 1.2 slice-start.3
  791.4 1.3 copy-start.5
  792.7 8.2 %copy-start.9 = (f32[640,256]{1,0:T(8,128)S(1)}, f32[640,256]{1,0:T(8,128)}, u32[]{:S(2)}) copy-start(f32[640,256]{1,0:T(8,128)} %copy.59) | copy-start | bytes 1966084
  792.7 8.2 %copy-start.17 = (f32[5,128,128]{2,1,0:T(8,128)S(1)}, f32[5,128,128]{2,1,0:T(8,128)}, u32[]{:S(2)}) copy-start(f32[5,128,128]{2,1,0:T(8,128)} %copy-done.16) | copy-start | bytes 983044
  792.7 9.3 %copy-start.8 = (f32[768,256]{1,0:T(8,128)S(1)}, f32[768,256]{1,0:T(8,128)}, u32[]{:S(2)}) copy-start(f32[768,256]{1,0:T(8,128)} %copy.60) | copy-start | bytes 2359300
  792.7 9.3 %copy-start.15 = (f32[6,128,128]{2,1,0:T(8,128)S(1)}, f32[6,128,128]{2,1,0:T(8,128)}, u32[]{:S(2)}) copy-start(f32[6,128,128]{2,1,0:T(8,128)} %copy-done.14) | copy-start | bytes 1179652
  794.6 8.6 %copy-start.7 = (f32[896,256]{1,0:T(8,128)S(1)}, f32[896,256]{1,0:T(8,128)}, u32[]{:S(2)}) copy-start(f32[896,256]{1,0:T(8,128)} %copy.61) | copy-start | bytes 2752516
  794.6 8.6 %copy-start.13 = (f32[7,128,128]{2,1,0:T(8,128)S(1)}, f32[7,128,128]{2,1,0:T(8,128)}, u32[]{:S(2)}) copy-start(f32[7,128,128]{2,1,0:T(8,128)} %copy-done.12) | copy-start | bytes 1376260
  802.0 3.8 copy-start.11
Sparse Core Ops, SparseCore 0:
  14.7 98.5 all-gather.2
  569.4 132.6 all-reduce.1
  761.1 23.8 all-gather.4
where the time goes:
time: 827 us; the launch traced here: 815 us
  matrix products  447 us (54%)
  waiting for transfers between devices  303 us (37%)
  local copies, waits for them, and re-layouts  37.9 us (5%)
  between operations  13.4 us (2%)
  other arithmetic  9.36 us (1%)
    dot_general x252, matrix products, compose(): jnp.einsum('kab,kbc->ac', left_tiles, right_tiles, precision=highest, pre...  433 us
    psum x1, waiting for transfers between devices, broadcast(): return lax.psum(kept, axis)  132 us
    all_gather x1, waiting for transfers between devices, prefix(): gathered = lax.all_gather(part, axis)  94.2 us
    ppermute x3, waiting for transfers between devices, passed_along(): lax.ppermute(value, axis, [(source, source + steps) for source in range(l...  52.2 us
    all_gather x1, waiting for transfers between devices, shards(): column_piece = lax.all_gather(entering, 'inner', axis=1, tiled=True)  24.1 us
    gather x7, local copies, waits for them, and re-layouts, compose(): by_column = earlier[column_order(tile_count)]  18.1 us
  transfers between devices with their start and end apart: 6, of which 6 were waited for; matrix products, arithmetic and copies ran while one was open for 0% of the time, Pallas kernels for 0%

commit v1 on v0

v1 whole, which is shorter than its diff:
```python
import functools

import jax
import jax.numpy as jnp
from jax import lax
from jax.experimental import pallas as pl
from jax.experimental.pallas import tpu as pltpu
from jax.sharding import PartitionSpec as P

MESH = pl.DeviceIdType.MESH


def split(x):
    hi = x.astype(jnp.bfloat16)
    lo = (x - hi.astype(jnp.float32)).astype(jnp.bfloat16)
    return hi, lo


def packed(i, j):
    return i * (i + 1) // 2 + j


def dot(a, b):
    return jnp.dot(a, b, preferred_element_type=jnp.float32)


def kernel(
    n_inner, total, nt, t, nc, w,
    pattern, coupling, log_diag, boundary, out,
    own, other, own_log, other_log, lhs, rhs, scale, state, expanded, result,
    load_sem, log_sem, pair_send, pair_recv, log_send, log_recv,
    chain_send, chain_recv, fwd_send, first_sem, out_sem,
):
    me = lax.axis_index("outer") * n_inner + lax.axis_index("inner")
    odd = lax.rem(me, 2) == 1
    even = jnp.logical_not(odd)
    composed = jnp.logical_and(odd, me > 1)
    has_next = jnp.logical_or(me == 0, jnp.logical_and(odd, me + 2 < total))
    after = jnp.where(me == 0, 1, lax.rem(me + 2, total))
    partner = jnp.where(odd, me - 1, me + 1)
    before = lax.rem(me + total - 2, total)

    def at(index):
        return {"outer": index // n_inner, "inner": lax.rem(index, n_inner)}

    def rows(i):
        return pl.ds(i * t, t)

    def load_row(i):
        part = pl.ds(packed(i, 0), i + 1)
        return pltpu.make_async_copy(coupling.at[part], own.at[part], load_sem.at[i])

    def pair_row(i):
        part = pl.ds(packed(i, 0), i + 1)
        return pltpu.make_async_remote_copy(
            src_ref=coupling.at[part], dst_ref=other.at[part],
            send_sem=pair_send.at[i], recv_sem=pair_recv.at[i],
            device_id=at(partner), device_id_type=MESH,
        )

    def pair_log():
        return pltpu.make_async_remote_copy(
            src_ref=log_diag, dst_ref=other_log,
            send_sem=log_send, recv_sem=log_recv,
            device_id=at(partner), device_id_type=MESH,
        )

    def chain(i, c):
        return pltpu.make_async_remote_copy(
            src_ref=result.at[c, rows(i)], dst_ref=state.at[c, rows(i)],
            send_sem=chain_send.at[i, c], recv_sem=chain_recv.at[i, c],
            device_id=at(after), device_id_type=MESH,
        )

    def forward(i, c):
        return pltpu.make_async_remote_copy(
            src_ref=state.at[c, rows(i)], dst_ref=state.at[c, rows(i)],
            send_sem=fwd_send.at[i, c], recv_sem=chain_recv.at[i, c],
            device_id=at(partner), device_id_type=MESH,
        )

    def first(i, c):
        return pltpu.make_async_copy(
            boundary.at[rows(i), pl.ds(c * w, w)], state.at[c, rows(i)], first_sem.at[i, c]
        )

    def store(i, c):
        return pltpu.make_async_copy(
            result.at[c, rows(i)], out.at[rows(i), pl.ds(c * w, w)], out_sem.at[i, c]
        )

    for i in range(nt):
        load_row(i).start()
    pltpu.make_async_copy(log_diag, own_log, log_sem).start()

    @pl.when(me == 0)
    def _():
        for i in range(nt):
            for c in range(nc):
                first(i, c).start()

    barrier = pltpu.get_barrier_semaphore()
    pl.semaphore_signal(barrier, inc=1, device_id=at(partner), device_id_type=MESH)

    @pl.when(composed)
    def _():
        pl.semaphore_signal(barrier, inc=1, device_id=at(before), device_id_type=MESH)

    @pl.when(jnp.logical_and(odd, has_next))
    def _():
        pl.semaphore_signal(barrier, inc=1, device_id=at(after), device_id_type=MESH)

    greeted = 1 + composed.astype(jnp.int32) + jnp.logical_and(odd, has_next).astype(jnp.int32)
    pl.semaphore_wait(barrier, greeted)

    sends_pair = jnp.logical_and(even, me > 0)

    @pl.when(sends_pair)
    def _():
        pair_log().start()
        for i in range(nt):
            pair_row(i).start()

    def weight(i, j):
        return 1.0 if i == j else pattern[i, j].astype(jnp.float32)

    def put_lhs(i, j, tile):
        hi, lo = split(tile)
        lhs[rows(i), pl.ds(j * 3 * t, t)] = hi
        lhs[rows(i), pl.ds(j * 3 * t + t, t)] = hi
        lhs[rows(i), pl.ds(j * 3 * t + 2 * t, t)] = lo

    def growth(ref, i):
        return jnp.transpose(jnp.broadcast_to(jnp.exp(ref[pl.ds(i, 1), :]), (t, t)))

    pair = 2 if nt % 2 == 0 else 1
    zero = jnp.zeros((t, t), jnp.bfloat16)

    pltpu.make_async_copy(log_diag, own_log, log_sem).wait()
    for i in range(nt):
        scale[rows(i), :] = growth(own_log, i)
        load_row(i).wait()
        for j in range(i + 1):
            put_lhs(i, j, own[packed(i, j)] * weight(i, j))

    @pl.when(composed)
    def _():
        for i in range(0, nt, pair):
            for j in range(i + 1, i + pair):
                for p in range(3):
                    lhs[rows(i), pl.ds((j * 3 + p) * t, t)] = zero
                    rhs[pl.ds((i * 3 + p) * t, t), pl.ds(j * t, t)] = zero
        eye = lax.broadcasted_iota(jnp.int32, (t, t), 0) == lax.broadcasted_iota(jnp.int32, (t, t), 1)
        pair_log().wait_recv()
        for i in range(nt):
            pair_row(i).wait_recv()
            for j in range(i + 1):
                tile = other[packed(i, j)] * weight(i, j)
                if i == j:
                    grown = jnp.broadcast_to(jnp.exp(other_log[pl.ds(i, 1), :]), (t, t))
                    tile = tile + jnp.where(eye, grown, 0.0)
                hi, lo = split(tile)
                rhs[pl.ds(i * 3 * t, t), pl.ds(j * t, t)] = hi
                rhs[pl.ds(i * 3 * t + t, t), pl.ds(j * t, t)] = lo
                rhs[pl.ds(i * 3 * t + 2 * t, t), pl.ds(j * t, t)] = hi
            if i % pair == pair - 1:
                top = i - pair + 1
                for left in range(0, i + 1, pair):
                    deep = pl.ds(left * 3 * t, (i + 1 - left) * 3 * t)
                    block = dot(
                        lhs[pl.ds(top * t, pair * t), deep], rhs[deep, pl.ds(left * t, pair * t)]
                    )
                    for a in range(pair):
                        for b in range(pair):
                            r, s = top + a, left + b
                            if s <= r:
                                tile = block[a * t : (a + 1) * t, b * t : (b + 1) * t]
                                tile += scale[rows(r), :] * (other[packed(r, s)] * weight(r, s))
                                put_lhs(r, s, tile)
        for i in range(nt):
            scale[rows(i), :] = scale[rows(i), :] * growth(other_log, i)

    for i in range(nt):
        for c in range(nc):
            partial = None
            if i:
                partial = dot(lhs[rows(i), pl.ds(0, i * 3 * t)], expanded[c, pl.ds(0, i * 3 * t), :])

            @pl.when(me == 0)
            def _():
                first(i, c).wait()

            @pl.when(me > 0)
            def _():
                chain(i, c).wait_recv()

            @pl.when(composed)
            def _():
                forward(i, c).start()

            x = state[c, rows(i), :]
            hi, lo = split(x)
            piece = jnp.concatenate([hi, lo, hi], axis=0)
            expanded[c, pl.ds(i * 3 * t, 3 * t), :] = piece
            y = dot(lhs[rows(i), pl.ds(i * 3 * t, 3 * t)], piece) + scale[rows(i), :w] * x
            result[c, rows(i), :] = y if partial is None else y + partial

            @pl.when(has_next)
            def _():
                chain(i, c).start()

            store(i, c).start()

    for i in range(nt):
        for c in range(nc):
            store(i, c).wait()

            @pl.when(has_next)
            def _():
                chain(i, c).wait_send()

            @pl.when(composed)
            def _():
                forward(i, c).wait_send()

    @pl.when(sends_pair)
    def _():
        pair_log().wait_send()
        for i in range(nt):
            pair_row(i).wait_send()


def solution(mesh):
    n_inner, n_outer = mesh.shape["inner"], mesh.shape["outer"]

    def shards(coupling, log_diag, pattern, boundary):
        t = coupling.shape[-1]
        m, b = boundary.shape
        nt = m // t
        w = min(t, b)
        nc = b // w
        tiles = coupling.shape[2]
        dma = pltpu.SemaphoreType.DMA
        anywhere = pl.BlockSpec(memory_space=pl.ANY)
        result = pl.pallas_call(
            functools.partial(kernel, n_inner, n_inner * n_outer, nt, t, nc, w),
            out_shape=jax.ShapeDtypeStruct((m, b), jnp.float32),
            in_specs=[pl.BlockSpec(memory_space=pltpu.SMEM)] + [anywhere] * 3,
            out_specs=anywhere,
            scratch_shapes=[
                pltpu.VMEM((tiles, t, t), jnp.float32),
                pltpu.VMEM((tiles, t, t), jnp.float32),
                pltpu.VMEM((nt, t), jnp.float32),
                pltpu.VMEM((nt, t), jnp.float32),
                pltpu.VMEM((m, 3 * m), jnp.bfloat16),
                pltpu.VMEM((3 * m, m), jnp.bfloat16),
                pltpu.VMEM((m, t), jnp.float32),
                pltpu.VMEM((nc, m, w), jnp.float32),
                pltpu.VMEM((nc, 3 * m, w), jnp.bfloat16),
                pltpu.VMEM((nc, m, w), jnp.float32),
                dma((nt,)), dma, dma((nt,)), dma((nt,)), dma, dma,
                dma((nt, nc)), dma((nt, nc)), dma((nt, nc)), dma((nt, nc)), dma((nt, nc)),
            ],
            compiler_params=pltpu.CompilerParams(collective_id=0, has_side_effects=True),
        )(pattern, coupling[0, 0], log_diag.reshape(nt, t), boundary)
        return result[None, None]

    return jax.shard_map(
        shards,
        mesh=mesh,
        in_specs=(P("outer", "inner", None, None, None), P("outer", "inner", None), P(), P()),
        out_specs=P("outer", "inner", None, None),
        check_vma=False,
    )
```

time: 827 us -> 61.2 us (0.07); the launches traced: 815 us -> 61 us
  matrix products: 447 us -> 0 us
  waiting for transfers between devices: 303 us -> 0 us
  Pallas kernels: 0 us -> 58.7 us
  local copies, waits for them, and re-layouts: 37.9 us -> 2.26 us
  between operations: 13.4 us -> 0.01 us
  other arithmetic: 9.36 us -> 0 us
    dot_general x260 -> x0, matrix products: 447 us -> none  [the longest x252 433 us: compose(): jnp.einsum('kab,kbc->ac', left_tiles, right_tiles, precision=highest, pre...]
    psum x1 -> x0, waiting for transfers between devices: 132 us -> none  [broadcast(): return lax.psum(kept, axis)]
    all_gather x2 -> x0, waiting for transfers between devices: 118 us -> none  [the longest x1 94.2 us: prefix(): gathered = lax.all_gather(part, axis)]
    pallas_call x0 -> x1, Pallas kernels: none -> 58.7 us  [shards(): pl.pallas_call(functools.partial(kernel, n_inner, n_inner * n_outer, nt,...]
    ppermute x3 -> x0, waiting for transfers between devices: 52.2 us -> none  [passed_along(): lax.ppermute(value, axis, [(source, source + steps) for source in range(l...]
    gather x9 -> x0, local copies, waits for them, and re-layouts: 20.5 us -> none  [the longest x7 18.1 us: compose(): by_column = earlier[column_order(tile_count)]]
  transfers between devices with their start and end apart: 6 -> 0, of which waited for: 6 -> 0; matrix products, arithmetic and copies ran while one was open for 0% -> 0% of each run, Pallas kernels for 0% -> 0%
where the time goes in v1:
time: 61.2 us; the launch traced here: 61 us
  Pallas kernels  58.7 us (96%)
  local copies, waits for them, and re-layouts  2.26 us (4%)
    pallas_call x1, Pallas kernels, shards(): pl.pallas_call(functools.partial(kernel, n_inner, n_inner * n_outer, nt,...  58.7 us
    unnamed x1, local copies, waits for them, and re-layouts  2.26 us

profile of v1, /device:TPU:30, one launch (start us, length us, event | category | flops | bytes accessed | tf_op | source)
XLA Modules:
  0.0 61.0 jit_solution(17420284927881160577)
XLA Ops:
  0.0 58.7 %shard_map.46 = f32[1024,256]{1,0:T(8,128)} custom-call(s32[8,8]{1,0:T(8,128)} %pattern.1, f32[36,128,128]{2,1,0:T(8,128)} %bitcast.4, f32[8,128]{1,0:T(8,128)} %bitcast.5, f32[1024,256]{1,0:T(8,128)} %boundary.1), custom_call_target="tpu_custom_call" | custom-call | tf_op jit(solution)/shard_map/pallas_call | solution.py:245
  58.7 2.3 %copy.6 = f32[1,1,1024,256]{3,2,1,0:T(8,128)} copy(f32[1,1,1024,256]{3,2,1,0:T(8,128)} %bitcast.3) | data formatting | bytes 2097152

commit v2 on v1

v2 whole, which is shorter than its diff:
```python
import functools

import jax
import jax.numpy as jnp
from jax import lax
from jax.experimental import pallas as pl
from jax.experimental.pallas import tpu as pltpu
from jax.sharding import PartitionSpec as P

MESH = pl.DeviceIdType.MESH
FIRST_FAST = 4


def split(x):
    hi = x.astype(jnp.bfloat16)
    lo = (x - hi.astype(jnp.float32)).astype(jnp.bfloat16)
    return hi, lo


def packed(i, j):
    return i * (i + 1) // 2 + j


def dot(a, b):
    return jnp.dot(a, b, preferred_element_type=jnp.float32)


def kernel(
    n_inner, total, nt, t, nc, w,
    pattern, coupling, log_diag, boundary, out,
    own, other, third, own_log, other_log, third_log, sum_log,
    lhs, lhs4, rhs, scale, scale4, state, expanded, result, result4,
    load_sem, log_sem, pair_send, pair_recv, log_send, log_recv,
    help_send, help_recv, sum_send, sum_recv,
    chain_send, chain_recv, fwd_send, fast_send, first_sem, out_sem,
):
    me = lax.axis_index("outer") * n_inner + lax.axis_index("inner")
    odd = lax.rem(me, 2) == 1
    even = jnp.logical_not(odd)
    composed = jnp.logical_and(odd, me > 1)
    spot, place = lax.rem(me, 4), me // 4
    in_fast_pair = jnp.logical_and(place >= FIRST_FAST, place < total // 4 - 1)
    fast = jnp.logical_and(spot == 1, in_fast_pair)
    helper = jnp.logical_and(spot == 3, in_fast_pair)
    goes_on = jnp.logical_and(odd, jnp.logical_and(me + 2 < total, jnp.logical_not(helper)))
    has_next = jnp.logical_or(me == 0, goes_on)
    after = jnp.where(me == 0, 1, lax.rem(me + 2, total))
    fast_after = lax.rem(me + 4, total)
    partner = jnp.where(odd, me - 1, me + 1)
    back = jnp.where(jnp.logical_and(spot == 1, place > FIRST_FAST), 4, 2)
    before = lax.rem(me + total - back, total)
    pair = 2 if nt % 2 == 0 else 1
    last_group = nt - pair

    def at(index):
        return {"outer": index // n_inner, "inner": lax.rem(index, n_inner)}

    def rows(i):
        return pl.ds(i * t, t)

    def load_row(i):
        part = pl.ds(packed(i, 0), i + 1)
        return pltpu.make_async_copy(coupling.at[part], own.at[part], load_sem.at[i])

    def pair_row(i):
        part = pl.ds(packed(i, 0), i + 1)
        return pltpu.make_async_remote_copy(
            src_ref=coupling.at[part], dst_ref=other.at[part],
            send_sem=pair_send.at[i], recv_sem=pair_recv.at[i],
            device_id=at(partner), device_id_type=MESH,
        )

    def pair_log():
        return pltpu.make_async_remote_copy(
            src_ref=log_diag, dst_ref=other_log,
            send_sem=log_send, recv_sem=log_recv,
            device_id=at(partner), device_id_type=MESH,
        )

    def help_rows(top):
        part = pl.ds(packed(top, 0), packed(top + pair, 0) - packed(top, 0))
        return pltpu.make_async_remote_copy(
            src_ref=own.at[part], dst_ref=third.at[part],
            send_sem=help_send.at[top // pair], recv_sem=help_recv.at[top // pair],
            device_id=at(lax.rem(me + total - 2, total)), device_id_type=MESH,
        )

    def help_log():
        return pltpu.make_async_remote_copy(
            src_ref=sum_log, dst_ref=third_log, send_sem=sum_send, recv_sem=sum_recv,
            device_id=at(lax.rem(me + total - 2, total)), device_id_type=MESH,
        )

    def fast_chain(i, c):
        return pltpu.make_async_remote_copy(
            src_ref=result4.at[c, rows(i)], dst_ref=state.at[c, rows(i)],
            send_sem=fast_send.at[i, c], recv_sem=chain_recv.at[i, c],
            device_id=at(fast_after), device_id_type=MESH,
        )

    def chain(i, c):
        return pltpu.make_async_remote_copy(
            src_ref=result.at[c, rows(i)], dst_ref=state.at[c, rows(i)],
            send_sem=chain_send.at[i, c], recv_sem=chain_recv.at[i, c],
            device_id=at(after), device_id_type=MESH,
        )

    def forward(i, c):
        return pltpu.make_async_remote_copy(
            src_ref=state.at[c, rows(i)], dst_ref=state.at[c, rows(i)],
            send_sem=fwd_send.at[i, c], recv_sem=chain_recv.at[i, c],
            device_id=at(partner), device_id_type=MESH,
        )

    def first(i, c):
        return pltpu.make_async_copy(
            boundary.at[rows(i), pl.ds(c * w, w)], state.at[c, rows(i)], first_sem.at[i, c]
        )

    def store(i, c):
        return pltpu.make_async_copy(
            result.at[c, rows(i)], out.at[rows(i), pl.ds(c * w, w)], out_sem.at[i, c]
        )

    for i in range(nt):
        load_row(i).start()
    pltpu.make_async_copy(log_diag, own_log, log_sem).start()

    @pl.when(me == 0)
    def _():
        for i in range(nt):
            for c in range(nc):
                first(i, c).start()

    def weight(i, j):
        return 1.0 if i == j else pattern[i, j].astype(jnp.float32)

    def put_lhs(buf, i, j, tile):
        hi, lo = split(tile)
        buf[rows(i), pl.ds(j * 3 * t, t)] = hi
        buf[rows(i), pl.ds(j * 3 * t + t, t)] = hi
        buf[rows(i), pl.ds(j * 3 * t + 2 * t, t)] = lo

    def put_rhs(i, j, tile):
        hi, lo = split(tile)
        rhs[pl.ds(i * 3 * t, t), pl.ds(j * t, t)] = hi
        rhs[pl.ds(i * 3 * t + t, t), pl.ds(j * t, t)] = lo
        rhs[pl.ds(i * 3 * t + 2 * t, t), pl.ds(j * t, t)] = hi

    def growth(ref, i):
        return jnp.transpose(jnp.broadcast_to(jnp.exp(ref[pl.ds(i, 1), :]), (t, t)))

    def clear(buf):
        for i in range(0, nt, pair):
            for j in range(i + 1, i + pair):
                buf[rows(i), pl.ds(j * 3 * t, 3 * t)] = jnp.zeros((t, 3 * t), jnp.bfloat16)

    def prepare(i):
        scale[rows(i), :] = growth(own_log, i)
        load_row(i).wait()
        for j in range(i + 1):
            put_lhs(lhs, i, j, own[packed(i, j)] * weight(i, j))

    def multiply(buf, top, left_scale, right, keep):
        for left in range(0, top + pair, pair):
            deep = pl.ds(left * 3 * t, (top + pair - left) * 3 * t)
            block = dot(buf[pl.ds(top * t, pair * t), deep], rhs[deep, pl.ds(left * t, pair * t)])
            for a in range(pair):
                for b in range(pair):
                    r, s = top + a, left + b
                    if s <= r:
                        tile = block[a * t : (a + 1) * t, b * t : (b + 1) * t]
                        tile += left_scale[rows(r), :] * right(r, s)
                        put_lhs(buf, r, s, tile)
                        if keep:
                            own[packed(r, s)] = tile

    eye = lax.broadcasted_iota(jnp.int32, (t, t), 0) == lax.broadcasted_iota(jnp.int32, (t, t), 1)

    def compose_start():
        clear(lhs)
        for i in range(0, nt, pair):
            for j in range(i + 1, i + pair):
                rhs[pl.ds(i * 3 * t, 3 * t), pl.ds(j * t, t)] = jnp.zeros((3 * t, t), jnp.bfloat16)
        pair_log().wait_recv()
        sum_log[...] = own_log[...] + other_log[...]

    def compose(top):
        for i in range(top, top + pair):
            pair_row(i).wait_recv()
            for j in range(i + 1):
                tile = other[packed(i, j)] * weight(i, j)
                if i == j:
                    grown = jnp.broadcast_to(jnp.exp(other_log[pl.ds(i, 1), :]), (t, t))
                    tile = tile + jnp.where(eye, grown, 0.0)
                put_rhs(i, j, tile)
        multiply(lhs, top, scale, lambda r, s: other[packed(r, s)] * weight(r, s), True)
        for i in range(top, top + pair):
            scale[rows(i), :] = scale[rows(i), :] * growth(other_log, i)

    def compose_fast(top):
        help_rows(top).wait_recv()
        for i in range(top, top + pair):
            scale4[rows(i), :] = growth(third_log, i)
            for j in range(i + 1):
                put_lhs(lhs4, i, j, third[packed(i, j)])
        multiply(lhs4, top, scale4, lambda r, s: own[packed(r, s)], False)
        for i in range(top, top + pair):
            scale4[rows(i), :] = scale4[rows(i), :] * scale[rows(i), :]

    barrier = pltpu.get_barrier_semaphore()
    pl.semaphore_signal(barrier, inc=1, device_id=at(partner), device_id_type=MESH)

    @pl.when(composed)
    def _():
        pl.semaphore_signal(barrier, inc=1, device_id=at(before), device_id_type=MESH)

    @pl.when(goes_on)
    def _():
        pl.semaphore_signal(barrier, inc=1, device_id=at(after), device_id_type=MESH)

    @pl.when(fast)
    def _():
        pl.semaphore_signal(barrier, inc=1, device_id=at(fast_after), device_id_type=MESH)

    pltpu.make_async_copy(log_diag, own_log, log_sem).wait()
    prepare(0)

    greeted = 1 + composed.astype(jnp.int32) + goes_on.astype(jnp.int32) + fast.astype(jnp.int32)
    pl.semaphore_wait(barrier, greeted)

    sends_pair = jnp.logical_and(even, me > 0)

    @pl.when(sends_pair)
    def _():
        pair_log().start()
        for i in range(nt):
            pair_row(i).start()

    @pl.when(me > 1)
    def _():
        for i in range(1, nt):
            prepare(i)

    @pl.when(composed)
    def _():
        compose_start()

        @pl.when(helper)
        def _():
            help_log().start()

    @pl.when(jnp.logical_and(composed, me != 3))
    def _():
        for top in range(0, nt, pair):
            compose(top)

            @pl.when(helper)
            def _():
                help_rows(top).start()

    @pl.when(fast)
    def _():
        clear(lhs4)
        for i in range(nt):
            for j in range(i + 1):
                tile = own[packed(i, j)]
                if i == j:
                    tile = tile + jnp.where(eye, scale[rows(i), :], 0.0)
                put_rhs(i, j, tile)
        help_log().wait_recv()
        for top in range(0, last_group, pair):
            compose_fast(top)

    @pl.when(jnp.logical_and(fast, place != FIRST_FAST))
    def _():
        compose_fast(last_group)

    for i in range(nt):
        if i:
            @pl.when(me < 2)
            def _():
                prepare(i)

        if i % pair == 0:
            @pl.when(me == 3)
            def _():
                compose(i)

        if i == last_group:
            @pl.when(jnp.logical_and(fast, place == FIRST_FAST))
            def _():
                compose_fast(i)

        for c in range(nc):
            partial = None
            if i:
                deep = pl.ds(0, i * 3 * t)

                @pl.when(fast)
                def _():
                    result4[c, rows(i), :] = dot(lhs4[rows(i), deep], expanded[c, deep, :])

                partial = dot(lhs[rows(i), deep], expanded[c, deep, :])

            @pl.when(me == 0)
            def _():
                first(i, c).wait()

            @pl.when(me > 0)
            def _():
                chain(i, c).wait_recv()

            @pl.when(composed)
            def _():
                forward(i, c).start()

            x = state[c, rows(i), :]
            hi, lo = split(x)
            piece = jnp.concatenate([hi, lo, hi], axis=0)
            expanded[c, pl.ds(i * 3 * t, 3 * t), :] = piece
            tip = pl.ds(i * 3 * t, 3 * t)

            @pl.when(fast)
            def _():
                ahead = dot(lhs4[rows(i), tip], expanded[c, tip, :])
                ahead += scale4[rows(i), :w] * state[c, rows(i), :]
                if i:
                    ahead += result4[c, rows(i), :]
                result4[c, rows(i), :] = ahead
                fast_chain(i, c).start()

            y = dot(lhs[rows(i), tip], piece) + scale[rows(i), :w] * x
            result[c, rows(i), :] = y if partial is None else y + partial

            @pl.when(has_next)
            def _():
                chain(i, c).start()

            store(i, c).start()

    for i in range(nt):
        for c in range(nc):
            store(i, c).wait()

            @pl.when(has_next)
            def _():
                chain(i, c).wait_send()

            @pl.when(composed)
            def _():
                forward(i, c).wait_send()

            @pl.when(fast)
            def _():
                fast_chain(i, c).wait_send()

    @pl.when(sends_pair)
    def _():
        pair_log().wait_send()
        for i in range(nt):
            pair_row(i).wait_send()

    @pl.when(helper)
    def _():
        help_log().wait_send()
        for top in range(0, nt, pair):
            help_rows(top).wait_send()


def solution(mesh):
    n_inner, n_outer = mesh.shape["inner"], mesh.shape["outer"]

    def shards(coupling, log_diag, pattern, boundary):
        t = coupling.shape[-1]
        m, b = boundary.shape
        nt = m // t
        w = min(t, b)
        nc = b // w
        tiles = coupling.shape[2]
        dma = pltpu.SemaphoreType.DMA
        anywhere = pl.BlockSpec(memory_space=pl.ANY)
        result = pl.pallas_call(
            functools.partial(kernel, n_inner, n_inner * n_outer, nt, t, nc, w),
            out_shape=jax.ShapeDtypeStruct((m, b), jnp.float32),
            in_specs=[pl.BlockSpec(memory_space=pltpu.SMEM)] + [anywhere] * 3,
            out_specs=anywhere,
            scratch_shapes=[
                pltpu.VMEM((tiles, t, t), jnp.float32),
                pltpu.VMEM((tiles, t, t), jnp.float32),
                pltpu.VMEM((tiles, t, t), jnp.float32),
                pltpu.VMEM((nt, t), jnp.float32),
                pltpu.VMEM((nt, t), jnp.float32),
                pltpu.VMEM((nt, t), jnp.float32),
                pltpu.VMEM((nt, t), jnp.float32),
                pltpu.VMEM((m, 3 * m), jnp.bfloat16),
                pltpu.VMEM((m, 3 * m), jnp.bfloat16),
                pltpu.VMEM((3 * m, m), jnp.bfloat16),
                pltpu.VMEM((m, t), jnp.float32),
                pltpu.VMEM((m, t), jnp.float32),
                pltpu.VMEM((nc, m, w), jnp.float32),
                pltpu.VMEM((nc, 3 * m, w), jnp.bfloat16),
                pltpu.VMEM((nc, m, w), jnp.float32),
                pltpu.VMEM((nc, m, w), jnp.float32),
                dma((nt,)), dma, dma((nt,)), dma((nt,)), dma, dma,
                dma((nt,)), dma((nt,)), dma, dma,
                dma((nt, nc)), dma((nt, nc)), dma((nt, nc)), dma((nt, nc)), dma((nt, nc)), dma((nt, nc)),
            ],
            compiler_params=pltpu.CompilerParams(collective_id=0, has_side_effects=True),
        )(pattern, coupling[0, 0], log_diag.reshape(nt, t), boundary)
        return result[None, None]

    return jax.shard_map(
        shards,
        mesh=mesh,
        in_specs=(P("outer", "inner", None, None, None), P("outer", "inner", None), P(), P()),
        out_specs=P("outer", "inner", None, None),
        check_vma=False,
    )
```

time: 61.2 us -> 70 us (1.14)
  Pallas kernels: 58.7 us -> 67.5 us
    pallas_call x1, Pallas kernels: 58.7 us -> 67.5 us  [shards(): pl.pallas_call(functools.partial(kernel, n_inner, n_inner * n_outer, nt,...]
where the time goes in v2:
time: 70 us; the launch traced here: 69.8 us
  Pallas kernels  67.5 us (96%)
  local copies, waits for them, and re-layouts  2.26 us (3%)
    pallas_call x1, Pallas kernels, shards(): pl.pallas_call(functools.partial(kernel, n_inner, n_inner * n_outer, nt,...  67.5 us
    unnamed x1, local copies, waits for them, and re-layouts  2.26 us

profile of v2, /device:TPU:30, one launch (start us, length us, event | category | flops | bytes accessed | tf_op | source)
XLA Modules:
  0.0 69.8 jit_solution(12259962401243360093)
XLA Ops:
  0.0 67.5 %shard_map.46 = f32[1024,256]{1,0:T(8,128)} custom-call(s32[8,8]{1,0:T(8,128)} %pattern.1, f32[36,128,128]{2,1,0:T(8,128)} %bitcast.4, f32[8,128]{1,0:T(8,128)} %bitcast.5, f32[1024,256]{1,0:T(8,128)} %boundary.1), custom_call_target="tpu_custom_call" | custom-call | tf_op jit(solution)/shard_map/pallas_call | solution.py:383
  67.5 2.3 %copy.6 = f32[1,1,1024,256]{3,2,1,0:T(8,128)} copy(f32[1,1,1024,256]{3,2,1,0:T(8,128)} %bitcast.3) | data formatting | bytes 2097152

commit v3 on v2

--- a/solution.py
+++ b/solution.py
@@ -29,26 +29,36 @@
     n_inner, total, nt, t, nc, w,
     pattern, coupling, log_diag, boundary, out,
     own, other, third, own_log, other_log, third_log, sum_log,
-    lhs, lhs4, rhs, scale, scale4, state, expanded, result, result4,
+    lhs, rhs, scale, state, expanded, result,
     load_sem, log_sem, pair_send, pair_recv, log_send, log_recv,
     help_send, help_recv, sum_send, sum_recv,
-    chain_send, chain_recv, fwd_send, fast_send, first_sem, out_sem,
+    chain_send, chain_recv, fwd_send, first_sem, out_sem,
 ):
     me = lax.axis_index("outer") * n_inner + lax.axis_index("inner")
     odd = lax.rem(me, 2) == 1
     even = jnp.logical_not(odd)
     composed = jnp.logical_and(odd, me > 1)
     spot, place = lax.rem(me, 4), me // 4
-    in_fast_pair = jnp.logical_and(place >= FIRST_FAST, place < total // 4 - 1)
-    fast = jnp.logical_and(spot == 1, in_fast_pair)
-    helper = jnp.logical_and(spot == 3, in_fast_pair)
-    goes_on = jnp.logical_and(odd, jnp.logical_and(me + 2 < total, jnp.logical_not(helper)))
-    has_next = jnp.logical_or(me == 0, goes_on)
-    after = jnp.where(me == 0, 1, lax.rem(me + 2, total))
-    fast_after = lax.rem(me + 4, total)
+    last = total // 4 - 1
+
+    def is_fast(index):
+        return jnp.logical_and(index >= FIRST_FAST, index < last)
+
+    fast_pair = is_fast(place)
+    slow_pair = jnp.logical_not(fast_pair)
+    fast = jnp.logical_and(spot == 3, fast_pair)
+    helper = jnp.logical_and(spot == 1, fast_pair)
+    leaves = jnp.logical_and(spot == 3, place < last)
+    has_next = jnp.logical_or(jnp.logical_or(me == 0, spot == 1), leaves)
+    step = jnp.where(spot == 1, jnp.where(fast_pair, 1, 2), jnp.where(is_fast(place + 1), 4, 2))
+    after = jnp.where(me == 0, 1, lax.rem(me + step, total))
     partner = jnp.where(odd, me - 1, me + 1)
-    back = jnp.where(jnp.logical_and(spot == 1, place > FIRST_FAST), 4, 2)
-    before = lax.rem(me + total - back, total)
+    target = jnp.where(fast, me - 2, partner)
+    before = lax.rem(me + total - jnp.where(fast, 4, 2), total)
+    other_chip = jnp.where(spot == 1, me + 2, lax.rem(me + total - 2, total))
+    cross = jnp.where(spot == 1, me + 1, lax.rem(me + total - 1, total))
+    enters = jnp.logical_or(fast, jnp.logical_and(spot == 1, jnp.logical_and(slow_pair, me > 1)))
+    crosses = jnp.logical_and(fast_pair, jnp.logical_or(spot == 1, spot == 2))
     pair = 2 if nt % 2 == 0 else 1
     last_group = nt - pair
 
@@ -82,20 +92,13 @@
         return pltpu.make_async_remote_copy(
             src_ref=own.at[part], dst_ref=third.at[part],
             send_sem=help_send.at[top // pair], recv_sem=help_recv.at[top // pair],
-            device_id=at(lax.rem(me + total - 2, total)), device_id_type=MESH,
+            device_id=at(other_chip), device_id_type=MESH,
         )
 
     def help_log():
         return pltpu.make_async_remote_copy(
             src_ref=sum_log, dst_ref=third_log, send_sem=sum_send, recv_sem=sum_recv,
-            device_id=at(lax.rem(me + total - 2, total)), device_id_type=MESH,
-        )
-
-    def fast_chain(i, c):
-        return pltpu.make_async_remote_copy(
-            src_ref=result4.at[c, rows(i)], dst_ref=state.at[c, rows(i)],
-            send_sem=fast_send.at[i, c], recv_sem=chain_recv.at[i, c],
-            device_id=at(fast_after), device_id_type=MESH,
+            device_id=at(other_chip), device_id_type=MESH,
         )
 
     def chain(i, c):
@@ -109,7 +112,7 @@
         return pltpu.make_async_remote_copy(
             src_ref=state.at[c, rows(i)], dst_ref=state.at[c, rows(i)],
             send_sem=fwd_send.at[i, c], recv_sem=chain_recv.at[i, c],
-            device_id=at(partner), device_id_type=MESH,
+            device_id=at(target), device_id_type=MESH,
         )
 
     def first(i, c):
@@ -201,32 +204,30 @@
     def compose_fast(top):
         help_rows(top).wait_recv()
         for i in range(top, top + pair):
-            scale4[rows(i), :] = growth(third_log, i)
+            grown = growth(third_log, i)
             for j in range(i + 1):
-                put_lhs(lhs4, i, j, third[packed(i, j)])
-        multiply(lhs4, top, scale4, lambda r, s: own[packed(r, s)], False)
+                tile = third[packed(i, j)]
+                if i == j:
+                    tile = tile + jnp.where(eye, grown, 0.0)
+                put_rhs(i, j, tile)
+        multiply(lhs, top, scale, lambda r, s: third[packed(r, s)], False)
         for i in range(top, top + pair):
-            scale4[rows(i), :] = scale4[rows(i), :] * scale[rows(i), :]
+            scale[rows(i), :] = scale[rows(i), :] * growth(third_log, i)
 
     barrier = pltpu.get_barrier_semaphore()
     pl.semaphore_signal(barrier, inc=1, device_id=at(partner), device_id_type=MESH)
 
-    @pl.when(composed)
-    def _():
-        pl.semaphore_signal(barrier, inc=1, device_id=at(before), device_id_type=MESH)
-
-    @pl.when(goes_on)
-    def _():
-        pl.semaphore_signal(barrier, inc=1, device_id=at(after), device_id_type=MESH)
-
-    @pl.when(fast)
-    def _():
-        pl.semaphore_signal(barrier, inc=1, device_id=at(fast_after), device_id_type=MESH)
+    for met, whom in ((odd, other_chip), (enters, before), (leaves, after), (crosses, cross)):
+        @pl.when(met)
+        def _():
+            pl.semaphore_signal(barrier, inc=1, device_id=at(whom), device_id_type=MESH)
 
     pltpu.make_async_copy(log_diag, own_log, log_sem).wait()
     prepare(0)
 
-    greeted = 1 + composed.astype(jnp.int32) + goes_on.astype(jnp.int32) + fast.astype(jnp.int32)
+    greeted = 1
+    for met in (odd, enters, leaves, crosses):
+        greeted = greeted + met.astype(jnp.int32)
     pl.semaphore_wait(barrier, greeted)
 
     sends_pair = jnp.logical_and(even, me > 0)
@@ -261,21 +262,10 @@
 
     @pl.when(fast)
     def _():
-        clear(lhs4)
-        for i in range(nt):
-            for j in range(i + 1):
-                tile = own[packed(i, j)]
-                if i == j:
-                    tile = tile + jnp.where(eye, scale[rows(i), :], 0.0)
-                put_rhs(i, j, tile)
         help_log().wait_recv()
         for top in range(0, last_group, pair):
             compose_fast(top)
 
-    @pl.when(jnp.logical_and(fast, place != FIRST_FAST))
-    def _():
-        compose_fast(last_group)
-
     for i in range(nt):
         if i:
             @pl.when(me < 2)
@@ -288,21 +278,17 @@
                 compose(i)
 
         if i == last_group:
-            @pl.when(jnp.logical_and(fast, place == FIRST_FAST))
+            @pl.when(fast)
             def _():
                 compose_fast(i)
 
+        if i:
+            deep = pl.ds(0, i * 3 * t)
+            partial = dot(lhs[rows(i), deep], expanded[deep, :])
+            for c in range(nc):
+                result[c, rows(i), :] = partial[:, c * w : (c + 1) * w]
+
         for c in range(nc):
-            partial = None
-            if i:
-                deep = pl.ds(0, i * 3 * t)
-
-                @pl.when(fast)
-                def _():
-                    result4[c, rows(i), :] = dot(lhs4[rows(i), deep], expanded[c, deep, :])
-
-                partial = dot(lhs[rows(i), deep], expanded[c, deep, :])
-
             @pl.when(me == 0)
             def _():
                 first(i, c).wait()
@@ -318,20 +304,12 @@
             x = state[c, rows(i), :]
             hi, lo = split(x)
             piece = jnp.concatenate([hi, lo, hi], axis=0)
-            expanded[c, pl.ds(i * 3 * t, 3 * t), :] = piece
+            expanded[pl.ds(i * 3 * t, 3 * t), pl.ds(c * w, w)] = piece
             tip = pl.ds(i * 3 * t, 3 * t)
-
-            @pl.when(fast)
-            def _():
-                ahead = dot(lhs4[rows(i), tip], expanded[c, tip, :])
-                ahead += scale4[rows(i), :w] * state[c, rows(i), :]
-                if i:
-                    ahead += result4[c, rows(i), :]
-                result4[c, rows(i), :] = ahead
-                fast_chain(i, c).start()
-
             y = dot(lhs[rows(i), tip], piece) + scale[rows(i), :w] * x
-            result[c, rows(i), :] = y if partial is None else y + partial
+            if i:
+                y += result[c, rows(i), :]
+            result[c, rows(i), :] = y
 
             @pl.when(has_next)
             def _():
@@ -350,10 +328,6 @@
             @pl.when(composed)
             def _():
                 forward(i, c).wait_send()
-
-            @pl.when(fast)
-            def _():
-                fast_chain(i, c).wait_send()
 
     @pl.when(sends_pair)
     def _():
@@ -394,17 +368,14 @@
                 pltpu.VMEM((nt, t), jnp.float32),
                 pltpu.VMEM((nt, t), jnp.float32),
                 pltpu.VMEM((m, 3 * m), jnp.bfloat16),
-                pltpu.VMEM((m, 3 * m), jnp.bfloat16),
                 pltpu.VMEM((3 * m, m), jnp.bfloat16),
                 pltpu.VMEM((m, t), jnp.float32),
-                pltpu.VMEM((m, t), jnp.float32),
                 pltpu.VMEM((nc, m, w), jnp.float32),
-                pltpu.VMEM((nc, 3 * m, w), jnp.bfloat16),
-                pltpu.VMEM((nc, m, w), jnp.float32),
+                pltpu.VMEM((3 * m, b), jnp.bfloat16),
                 pltpu.VMEM((nc, m, w), jnp.float32),
                 dma((nt,)), dma, dma((nt,)), dma((nt,)), dma, dma,
                 dma((nt,)), dma((nt,)), dma, dma,
-                dma((nt, nc)), dma((nt, nc)), dma((nt, nc)), dma((nt, nc)), dma((nt, nc)), dma((nt, nc)),
+                dma((nt, nc)), dma((nt, nc)), dma((nt, nc)), dma((nt, nc)), dma((nt, nc)),
             ],
             compiler_params=pltpu.CompilerParams(collective_id=0, has_side_effects=True),
         )(pattern, coupling[0, 0], log_diag.reshape(nt, t), boundary)

time: 70 us -> 61.4 us (0.88)
  Pallas kernels: 67.5 us -> 58.9 us
    pallas_call x1, Pallas kernels: 67.5 us -> 58.9 us  [shards(): pl.pallas_call(functools.partial(kernel, n_inner, n_inner * n_outer, nt,...]
where the time goes in v3:
time: 61.4 us; the launch traced here: 61.2 us
  Pallas kernels  58.9 us (96%)
  local copies, waits for them, and re-layouts  2.26 us (4%)
    pallas_call x1, Pallas kernels, shards(): pl.pallas_call(functools.partial(kernel, n_inner, n_inner * n_outer, nt,...  58.9 us
    unnamed x1, local copies, waits for them, and re-layouts  2.26 us

profile of v3, /device:TPU:30, one launch (start us, length us, event | category | flops | bytes accessed | tf_op | source)
XLA Modules:
  0.0 61.2 jit_solution(8478927067845203824)
XLA Ops:
  0.0 58.9 %shard_map.46 = f32[1024,256]{1,0:T(8,128)} custom-call(s32[8,8]{1,0:T(8,128)} %pattern.1, f32[36,128,128]{2,1,0:T(8,128)} %bitcast.4, f32[8,128]{1,0:T(8,128)} %bitcast.5, f32[1024,256]{1,0:T(8,128)} %boundary.1), custom_call_target="tpu_custom_call" | custom-call | tf_op jit(solution)/shard_map/pallas_call | solution.py:357
  59.0 2.3 %copy.6 = f32[1,1,1024,256]{3,2,1,0:T(8,128)} copy(f32[1,1,1024,256]{3,2,1,0:T(8,128)} %bitcast.3) | data formatting | bytes 2097152

commit v4 on v3

--- a/solution.py
+++ b/solution.py
@@ -42,7 +42,7 @@
     last = total // 4 - 1
 
     def is_fast(index):
-        return jnp.logical_and(index >= FIRST_FAST, index < last)
+        return jnp.logical_and(index >= FIRST_FAST, index <= last)
 
     fast_pair = is_fast(place)
     slow_pair = jnp.logical_not(fast_pair)

time: 61.4 us -> 54 us (0.88)
  Pallas kernels: 58.9 us -> 51.6 us
    pallas_call x1, Pallas kernels: 58.9 us -> 51.6 us  [shards(): pl.pallas_call(functools.partial(kernel, n_inner, n_inner * n_outer, nt,...]
where the time goes in v4:
time: 54 us; the launch traced here: 53.8 us
  Pallas kernels  51.6 us (96%)
  local copies, waits for them, and re-layouts  2.26 us (4%)
    pallas_call x1, Pallas kernels, shards(): pl.pallas_call(functools.partial(kernel, n_inner, n_inner * n_outer, nt,...  51.6 us
    unnamed x1, local copies, waits for them, and re-layouts  2.26 us

profile of v4, /device:TPU:30, one launch (start us, length us, event | category | flops | bytes accessed | tf_op | source)
XLA Modules:
  0.0 53.8 jit_solution(2812176175038483663)
XLA Ops:
  0.0 51.6 %shard_map.46 = f32[1024,256]{1,0:T(8,128)} custom-call(s32[8,8]{1,0:T(8,128)} %pattern.1, f32[36,128,128]{2,1,0:T(8,128)} %bitcast.4, f32[8,128]{1,0:T(8,128)} %bitcast.5, f32[1024,256]{1,0:T(8,128)} %boundary.1), custom_call_target="tpu_custom_call" | custom-call | tf_op jit(solution)/shard_map/pallas_call | solution.py:357
  51.6 2.3 %copy.6 = f32[1,1,1024,256]{3,2,1,0:T(8,128)} copy(f32[1,1,1024,256]{3,2,1,0:T(8,128)} %bitcast.3) | data formatting | bytes 2097152

commit v5 on v4

--- a/solution.py
+++ b/solution.py
@@ -32,7 +32,7 @@
     lhs, rhs, scale, state, expanded, result,
     load_sem, log_sem, pair_send, pair_recv, log_send, log_recv,
     help_send, help_recv, sum_send, sum_recv,
-    chain_send, chain_recv, fwd_send, first_sem, out_sem,
+    chain_send, chain_recv, fwd_send, beside_send, first_sem, out_sem,
 ):
     me = lax.axis_index("outer") * n_inner + lax.axis_index("inner")
     odd = lax.rem(me, 2) == 1
@@ -49,16 +49,15 @@
     fast = jnp.logical_and(spot == 3, fast_pair)
     helper = jnp.logical_and(spot == 1, fast_pair)
     leaves = jnp.logical_and(spot == 3, place < last)
-    has_next = jnp.logical_or(jnp.logical_or(me == 0, spot == 1), leaves)
-    step = jnp.where(spot == 1, jnp.where(fast_pair, 1, 2), jnp.where(is_fast(place + 1), 4, 2))
+    beside = jnp.logical_and(spot == 2, fast_pair)
+    has_next = jnp.logical_or(me == 0, jnp.logical_or(jnp.logical_and(spot == 1, slow_pair), leaves))
+    step = jnp.where(spot == 1, 2, jnp.where(is_fast(place + 1), 4, 2))
     after = jnp.where(me == 0, 1, lax.rem(me + step, total))
     partner = jnp.where(odd, me - 1, me + 1)
     target = jnp.where(fast, me - 2, partner)
     before = lax.rem(me + total - jnp.where(fast, 4, 2), total)
     other_chip = jnp.where(spot == 1, me + 2, lax.rem(me + total - 2, total))
-    cross = jnp.where(spot == 1, me + 1, lax.rem(me + total - 1, total))
     enters = jnp.logical_or(fast, jnp.logical_and(spot == 1, jnp.logical_and(slow_pair, me > 1)))
-    crosses = jnp.logical_and(fast_pair, jnp.logical_or(spot == 1, spot == 2))
     pair = 2 if nt % 2 == 0 else 1
     last_group = nt - pair
 
@@ -99,6 +98,27 @@
         return pltpu.make_async_remote_copy(
             src_ref=sum_log, dst_ref=third_log, send_sem=sum_send, recv_sem=sum_recv,
             device_id=at(other_chip), device_id_type=MESH,
+        )
+
+    def relay_rows(top):
+        part = pl.ds(packed(top, 0), packed(top + pair, 0) - packed(top, 0))
+        return pltpu.make_async_remote_copy(
+            src_ref=third.at[part], dst_ref=third.at[part],
+            send_sem=help_send.at[top // pair], recv_sem=help_recv.at[top // pair],
+            device_id=at(partner), device_id_type=MESH,
+        )
+
+    def relay_log():
+        return pltpu.make_async_remote_copy(
+            src_ref=third_log, dst_ref=third_log, send_sem=sum_send, recv_sem=sum_recv,
+            device_id=at(partner), device_id_type=MESH,
+        )
+
+    def beside_chain(i, c):
+        return pltpu.make_async_remote_copy(
+            src_ref=state.at[c, rows(i)], dst_ref=state.at[c, rows(i)],
+            send_sem=beside_send.at[i, c], recv_sem=chain_recv.at[i, c],
+            device_id=at(partner), device_id_type=MESH,
         )
 
     def chain(i, c):
@@ -180,11 +200,14 @@
 
     eye = lax.broadcasted_iota(jnp.int32, (t, t), 0) == lax.broadcasted_iota(jnp.int32, (t, t), 1)
 
-    def compose_start():
+    def clear_both():
         clear(lhs)
         for i in range(0, nt, pair):
             for j in range(i + 1, i + pair):
                 rhs[pl.ds(i * 3 * t, 3 * t), pl.ds(j * t, t)] = jnp.zeros((3 * t, t), jnp.bfloat16)
+
+    def compose_start():
+        clear_both()
         pair_log().wait_recv()
         sum_log[...] = own_log[...] + other_log[...]
 
@@ -203,6 +226,11 @@
 
     def compose_fast(top):
         help_rows(top).wait_recv()
+
+        @pl.when(fast)
+        def _():
+            relay_rows(top).start()
+
         for i in range(top, top + pair):
             grown = growth(third_log, i)
             for j in range(i + 1):
@@ -217,7 +245,7 @@
     barrier = pltpu.get_barrier_semaphore()
     pl.semaphore_signal(barrier, inc=1, device_id=at(partner), device_id_type=MESH)
 
-    for met, whom in ((odd, other_chip), (enters, before), (leaves, after), (crosses, cross)):
+    for met, whom in ((odd, other_chip), (enters, before), (leaves, after)):
         @pl.when(met)
         def _():
             pl.semaphore_signal(barrier, inc=1, device_id=at(whom), device_id_type=MESH)
@@ -226,7 +254,7 @@
     prepare(0)
 
     greeted = 1
-    for met in (odd, enters, leaves, crosses):
+    for met in (odd, enters, leaves):
         greeted = greeted + met.astype(jnp.int32)
     pl.semaphore_wait(barrier, greeted)
 
@@ -260,9 +288,18 @@
             def _():
                 help_rows(top).start()
 
-    @pl.when(fast)
+    @pl.when(beside)
+    def _():
+        clear_both()
+
+    @pl.when(jnp.logical_or(fast, beside))
     def _():
         help_log().wait_recv()
+
+        @pl.when(fast)
+        def _():
+            relay_log().start()
+
         for top in range(0, last_group, pair):
             compose_fast(top)
 
@@ -278,7 +315,7 @@
                 compose(i)
 
         if i == last_group:
-            @pl.when(fast)
+            @pl.when(jnp.logical_or(fast, beside))
             def _():
                 compose_fast(i)
 
@@ -300,6 +337,10 @@
             @pl.when(composed)
             def _():
                 forward(i, c).start()
+
+            @pl.when(fast)
+            def _():
+                beside_chain(i, c).start()
 
             x = state[c, rows(i), :]
             hi, lo = split(x)
@@ -329,6 +370,10 @@
             def _():
                 forward(i, c).wait_send()
 
+            @pl.when(fast)
+            def _():
+                beside_chain(i, c).wait_send()
+
     @pl.when(sends_pair)
     def _():
         pair_log().wait_send()
@@ -340,6 +385,12 @@
         help_log().wait_send()
         for top in range(0, nt, pair):
             help_rows(top).wait_send()
+
+    @pl.when(fast)
+    def _():
+        relay_log().wait_send()
+        for top in range(0, nt, pair):
+            relay_rows(top).wait_send()
 
 
 def solution(mesh):
@@ -375,7 +426,7 @@
                 pltpu.VMEM((nc, m, w), jnp.float32),
                 dma((nt,)), dma, dma((nt,)), dma((nt,)), dma, dma,
                 dma((nt,)), dma((nt,)), dma, dma,
-                dma((nt, nc)), dma((nt, nc)), dma((nt, nc)), dma((nt, nc)), dma((nt, nc)),
+                dma((nt, nc)), dma((nt, nc)), dma((nt, nc)), dma((nt, nc)), dma((nt, nc)), dma((nt, nc)),
             ],
             compiler_params=pltpu.CompilerParams(collective_id=0, has_side_effects=True),
         )(pattern, coupling[0, 0], log_diag.reshape(nt, t), boundary)

time: 54 us -> 52.1 us (0.965)
  the two profiles are of different devices: /device:TPU:30 before, /device:TPU:28 now
where the time goes in v5:
time: 52.1 us; the launch traced here: 51.9 us
  Pallas kernels  49.6 us (95%)
  local copies, waits for them, and re-layouts  2.26 us (4%)
    pallas_call x1, Pallas kernels, shards(): pl.pallas_call(functools.partial(kernel, n_inner, n_inner * n_outer, nt,...  49.6 us
    unnamed x1, local copies, waits for them, and re-layouts  2.26 us

profile of v5, /device:TPU:28, one launch (start us, length us, event | category | flops | bytes accessed | tf_op | source)
XLA Modules:
  0.0 51.9 jit_solution(12132443721833112707)
XLA Ops:
  0.0 49.6 %shard_map.46 = f32[1024,256]{1,0:T(8,128)} custom-call(s32[8,8]{1,0:T(8,128)} %pattern.1, f32[36,128,128]{2,1,0:T(8,128)} %bitcast.4, f32[8,128]{1,0:T(8,128)} %bitcast.5, f32[1024,256]{1,0:T(8,128)} %boundary.1), custom_call_target="tpu_custom_call" | custom-call | tf_op jit(solution)/shard_map/pallas_call | solution.py:408
  49.6 2.3 %copy.6 = f32[1,1,1024,256]{3,2,1,0:T(8,128)} copy(f32[1,1,1024,256]{3,2,1,0:T(8,128)} %bitcast.3) | data formatting | bytes 2097152

commit v6 on v5

--- a/solution.py
+++ b/solution.py
@@ -8,7 +8,7 @@
 from jax.sharding import PartitionSpec as P
 
 MESH = pl.DeviceIdType.MESH
-FIRST_FAST = 4
+FIRST_FAST = 3
 
 
 def split(x):

time: 52.1 us -> 53 us (1.017)
  Pallas kernels: 49.6 us -> 50.5 us
    pallas_call x1, Pallas kernels: 49.6 us -> 50.5 us  [shards(): pl.pallas_call(functools.partial(kernel, n_inner, n_inner * n_outer, nt,...]
where the time goes in v6:
time: 53 us; the launch traced here: 52.8 us
  Pallas kernels  50.5 us (95%)
  local copies, waits for them, and re-layouts  2.26 us (4%)
    pallas_call x1, Pallas kernels, shards(): pl.pallas_call(functools.partial(kernel, n_inner, n_inner * n_outer, nt,...  50.5 us
    unnamed x1, local copies, waits for them, and re-layouts  2.26 us

profile of v6, /device:TPU:28, one launch (start us, length us, event | category | flops | bytes accessed | tf_op | source)
XLA Modules:
  0.0 52.8 jit_solution(16787075573338263151)
XLA Ops:
  0.0 50.5 %shard_map.46 = f32[1024,256]{1,0:T(8,128)} custom-call(s32[8,8]{1,0:T(8,128)} %pattern.1, f32[36,128,128]{2,1,0:T(8,128)} %bitcast.4, f32[8,128]{1,0:T(8,128)} %bitcast.5, f32[1024,256]{1,0:T(8,128)} %boundary.1), custom_call_target="tpu_custom_call" | custom-call | tf_op jit(solution)/shard_map/pallas_call | solution.py:408
  50.5 2.3 %copy.6 = f32[1,1,1024,256]{3,2,1,0:T(8,128)} copy(f32[1,1,1024,256]{3,2,1,0:T(8,128)} %bitcast.3) | data formatting | bytes 2097152
